TPU v7x, 32 devices: a whole 2x2x4 slice. The times are simulated.
32 devices in a mesh: dp: 8 (over y, x, core), ctx: 4 (over z).
Axes of the slice: x: 2, y: 2, z: 4, core: 2. Of those that a mesh axis runs over, the one named last changes fastest.
Arguments:
- tokens: bfloat16 [16, 2048, 1088], P('dp', 'ctx'), may hold values from -6 to 6
- segments: int32 [16, 2048], P('dp'), may hold values from 0 to 31, never falling along the last dimension, each value on 1 to 1024 neighbouring positions
- adapter_index: int32 [16], P('dp'), may hold values from 0 to 7
- w_qkv: bfloat16 [1088, 3264], P('ctx', 'dp'), may hold values from -0.1875 to 0.1875
- w_out: bfloat16 [1088, 1088], P('ctx', 'dp'), may hold values from -0.75 to 0.75
- w_fc1: bfloat16 [1088, 4352], P('ctx', 'dp'), may hold values from -0.1875 to 0.1875
- w_fc2: bfloat16 [4352, 1088], P('ctx', 'dp'), may hold values from -0.09375 to 0.09375
- gain_one: float32 [1088], replicated, may hold values from 0.1 to 1.9
- gain_two: float32 [1088], replicated, may hold values from 0.1 to 1.9
- qkv_down: bfloat16 [128, 1088], replicated, may hold values from -0.1875 to 0.1875
- qkv_up: bfloat16 [128, 3264], replicated, may hold values from -0.75 to 0.75
- out_down: bfloat16 [128, 1088], replicated, may hold values from -0.1875 to 0.1875
- out_up: bfloat16 [128, 1088], replicated, may hold values from -0.75 to 0.75
- fc1_down: bfloat16 [128, 1088], replicated, may hold values from -0.1875 to 0.1875
- fc1_up: bfloat16 [128, 4352], replicated, may hold values from -0.75 to 0.75
- fc2_down: bfloat16 [128, 4352], replicated, may hold values from -0.09375 to 0.09375
- fc2_up: bfloat16 [128, 1088], replicated, may hold values from -0.75 to 0.75
- cotangent: bfloat16 [16, 2048, 1088], P('dp', 'ctx'), may hold values from -6 to 6
Outputs:
- output: bfloat16 [16, 2048, 1088], P('dp', 'ctx')
- input_grad: bfloat16 [16, 2048, 1088], P('dp', 'ctx')
- qkv_down_grad: float32 [128, 1088], P('dp', 'ctx')
- qkv_up_grad: float32 [128, 3264], P('dp', 'ctx')
- out_down_grad: float32 [128, 1088], P('dp', 'ctx')
- out_up_grad: float32 [128, 1088], P('dp', 'ctx')
- fc1_down_grad: float32 [128, 1088], P('dp', 'ctx')
- fc1_up_grad: float32 [128, 4352], P('dp', 'ctx')
- fc2_down_grad: float32 [128, 4352], P('dp', 'ctx')
- fc2_up_grad: float32 [128, 1088], P('dp', 'ctx')
Inputs may be any that keep to these rules, and one draw needn't show every extreme that they name: `segments`: document numbers never fall along a sequence; a document holds at most 1024 tokens.
All inputs are finite; a program needn't handle non-finite values.
Results may differ from a plain program's by a relative error of at most 0.023.
Values may be sent and summed in bfloat16 or wider, within the bound.
No kernel may reach another device: no remote copies, remote signals or barrier semaphores. Data moves between devices by JAX's collectives and lax.ppermute only.
A program may use at most 320 MiB of HBM per device.

v0:
```python
import jax
import jax.numpy as jnp
from jax import lax
from jax.sharding import PartitionSpec as P

HEADS = 17
ADAPTERS = 8
eps = 1e-05
neg_big = -1e30


def norm_rows(vector, gain):
    center = vector - jnp.mean(vector, -1, keepdims=True)
    inv_std = lax.rsqrt(jnp.mean(center * center, -1, keepdims=True) + eps)
    scaled = center * inv_std
    return (scaled * gain, scaled, inv_std)


def norm_back(grad, scaled, inv_std, gain):
    inner = grad * gain
    return inv_std * (
        inner
        - jnp.mean(inner, -1, keepdims=True)
        - scaled * jnp.mean(inner * scaled, -1, keepdims=True)
    )


def select_adapter(picker, stack):
    shaped = stack.reshape(picker.shape[1], stack.shape[0] // picker.shape[1], stack.shape[1])
    return jnp.einsum("sa,arw->srw", picker, shaped, preferred_element_type=jnp.float32).astype(
        jnp.bfloat16
    )


def project(inputs, weight, down_rows, up_rows):
    main_part = jnp.einsum("slw,wv->slv", inputs, weight, preferred_element_type=jnp.float32)
    lowered = jnp.einsum(
        "slw,srw->slr", inputs, down_rows, preferred_element_type=jnp.float32
    ).astype(jnp.bfloat16)
    return (
        main_part
        + jnp.einsum("slr,srv->slv", lowered, up_rows, preferred_element_type=jnp.float32),
        lowered,
    )


def project_back(grad_low, inputs, lowered, weight, down_rows, up_rows):
    grad_in = jnp.einsum("slv,wv->slw", grad_low, weight, preferred_element_type=jnp.float32)
    grad_mid = jnp.einsum(
        "slv,srv->slr", grad_low, up_rows, preferred_element_type=jnp.float32
    ).astype(jnp.bfloat16)
    grad_in = grad_in + jnp.einsum(
        "slr,srw->slw", grad_mid, down_rows, preferred_element_type=jnp.float32
    )
    grad_up = jnp.einsum("slr,slv->srv", lowered, grad_low, preferred_element_type=jnp.float32)
    grad_down = jnp.einsum("slr,slw->srw", grad_mid, inputs, preferred_element_type=jnp.float32)
    return (grad_in, grad_down, grad_up)


def gather_weights(part_qkv, part_out, part_fc1, part_fc2):
    wide_qkv, wide_out, wide_fc1, wide_fc2 = (
        lax.all_gather(part_qkv, "dp", axis=1, tiled=True),
        lax.all_gather(part_out, "dp", axis=1, tiled=True),
        lax.all_gather(part_fc1, "dp", axis=1, tiled=True),
        lax.all_gather(part_fc2, "dp", axis=1, tiled=True),
    )
    return (
        lax.all_gather(wide_qkv, "ctx", axis=0, tiled=True),
        lax.all_gather(wide_out, "ctx", axis=0, tiled=True),
        lax.all_gather(wide_fc1, "ctx", axis=0, tiled=True),
        lax.all_gather(wide_fc2, "ctx", axis=0, tiled=True),
    )


def block_mask(query_pos, query_seg, key_pos, key_seg):
    causal = key_pos[None, None, :] <= query_pos[None, :, None]
    same_doc = key_seg[:, None, :] == query_seg[:, :, None]
    return (causal & same_doc)[:, None]


def per_device(
    tokens,
    segments,
    adapter_index,
    w_qkv,
    w_out,
    w_fc1,
    w_fc2,
    gain_one,
    gain_two,
    qkv_down,
    qkv_up,
    out_down,
    out_up,
    fc1_down,
    fc1_up,
    fc2_down,
    fc2_up,
    cotangent,
):
    seq_count, row_count, width = tokens.shape
    head_dim = width // HEADS
    scale = head_dim ** (-0.5)
    full_qkv, full_out, full_fc1, full_fc2 = gather_weights(w_qkv, w_out, w_fc1, w_fc2)
    picker = (adapter_index[:, None] == jnp.arange(ADAPTERS, dtype=jnp.int32)[None, :]).astype(
        jnp.bfloat16
    )
    stacks = (qkv_down, qkv_up, out_down, out_up, fc1_down, fc1_up, fc2_down, fc2_up)
    chosen = [select_adapter(picker, stack) for stack in stacks]
    first_query = lax.axis_index("ctx") * row_count
    query_pos = first_query + jnp.arange(row_count, dtype=jnp.int32)
    query_seg = lax.dynamic_slice_in_dim(segments, first_query, row_count, 1)
    stream = tokens.astype(jnp.float32)
    normed_one, scaled_one, inv_one = norm_rows(stream, gain_one)
    normed_one = normed_one.astype(jnp.bfloat16)
    merged, lowered_qkv = project(normed_one, full_qkv, chosen[0], chosen[1])
    merged = merged.astype(jnp.bfloat16)
    queries = merged[..., :width].reshape(seq_count, row_count, HEADS, head_dim)
    key_vals = merged[..., width:]

    def attend(state, keys, values, mask):
        peak_old, total, accum = state
        scores = (
            jnp.einsum("sqhd,skhd->shqk", queries, keys, preferred_element_type=jnp.float32) * scale
        )
        scores = jnp.where(mask, scores, neg_big)
        peak_new = jnp.maximum(peak_old, jnp.max(scores, -1))
        expo_term = jnp.where(mask, jnp.exp(scores - peak_new[..., None]), 0.0)
        fade = jnp.exp(peak_old - peak_new)
        total = total * fade + jnp.sum(expo_term, -1)
        accum = accum * jnp.swapaxes(fade, 1, 2)[..., None] + jnp.einsum(
            "shqk,skhd->sqhd",
            expo_term.astype(jnp.bfloat16),
            values,
            preferred_element_type=jnp.float32,
        )
        return (peak_new, total, accum)

    start_state = (
        jnp.full((seq_count, HEADS, row_count), neg_big, jnp.float32),
        jnp.zeros((seq_count, HEADS, row_count), jnp.float32),
        jnp.zeros((seq_count, row_count, HEADS, head_dim), jnp.float32),
    )
    piece = lax.all_gather(key_vals, "ctx", axis=1, tiled=True)
    key_count = piece.shape[1]
    block = 512

    def key_step(turn, inner):
        offset = turn * block
        part = lax.dynamic_slice_in_dim(piece, turn * block, block, 1)
        key_pos = offset + jnp.arange(block, dtype=jnp.int32)
        key_seg = lax.dynamic_slice_in_dim(segments, offset, block, 1)
        mask = block_mask(query_pos, query_seg, key_pos, key_seg)
        keys = part[..., :width].reshape(seq_count, block, HEADS, head_dim)
        values = part[..., width:].reshape(seq_count, block, HEADS, head_dim)
        return attend(inner, keys, values, mask)

    peak_end, total_end, accum_end = lax.fori_loop(0, key_count // block, key_step, start_state)
    attended = (accum_end / jnp.swapaxes(total_end, 1, 2)[..., None]).reshape(
        seq_count, row_count, width
    )
    log_total = peak_end + jnp.log(total_end)
    attended_low = attended.astype(jnp.bfloat16)
    branch, lowered_out = project(attended_low, full_out, chosen[2], chosen[3])
    middle = stream + branch
    normed_two, scaled_two, inv_two = norm_rows(middle, gain_two)
    normed_two = normed_two.astype(jnp.bfloat16)
    hidden, lowered_fc1 = project(normed_two, full_fc1, chosen[4], chosen[5])
    active = jax.nn.gelu(hidden, approximate=True).astype(jnp.bfloat16)
    mlp_out, lowered_fc2 = project(active, full_fc2, chosen[6], chosen[7])
    output = (middle + mlp_out).astype(jnp.bfloat16)
    full_qkv, full_out, full_fc1, full_fc2 = gather_weights(w_qkv, w_out, w_fc1, w_fc2)
    grad_active, grad_fc2_down, grad_fc2_up = project_back(
        cotangent, active, lowered_fc2, full_fc2, chosen[6], chosen[7]
    )
    gelu_value, gelu_pull = jax.vjp(
        lambda inner_in: jax.nn.gelu(inner_in, approximate=True), hidden
    )
    grad_hidden = gelu_pull(grad_active)[0].astype(jnp.bfloat16)
    grad_two, grad_fc1_down, grad_fc1_up = project_back(
        grad_hidden, normed_two, lowered_fc1, full_fc1, chosen[4], chosen[5]
    )
    grad_middle = cotangent.astype(jnp.float32) + norm_back(grad_two, scaled_two, inv_two, gain_two)
    grad_branch = grad_middle.astype(jnp.bfloat16)
    grad_att, grad_out_down, grad_out_up = project_back(
        grad_branch, attended_low, lowered_out, full_out, chosen[2], chosen[3]
    )
    grad_att = grad_att.astype(jnp.bfloat16)
    grad_att_heads = grad_att.reshape(seq_count, row_count, HEADS, head_dim)
    delta = jnp.swapaxes(
        jnp.sum(
            (grad_att.astype(jnp.float32) * attended).reshape(
                seq_count, row_count, HEADS, head_dim
            ),
            -1,
        ),
        1,
        2,
    )
    all_keys = lax.all_gather(key_vals, "ctx", axis=1, tiled=True)
    key_total = all_keys.shape[1]
    back_block = 512

    def back_step(turn, state):
        offset = turn * back_block
        part = lax.dynamic_slice_in_dim(all_keys, offset, back_block, 1)
        key_pos = offset + jnp.arange(back_block, dtype=jnp.int32)
        key_seg = lax.dynamic_slice_in_dim(segments, offset, back_block, 1)
        mask = block_mask(query_pos, query_seg, key_pos, key_seg)
        keys = part[..., :width].reshape(seq_count, back_block, HEADS, head_dim)
        values = part[..., width:].reshape(seq_count, back_block, HEADS, head_dim)
        grad_query, grad_keys = state
        scores = (
            jnp.einsum("sqhd,skhd->shqk", queries, keys, preferred_element_type=jnp.float32) * scale
        )
        probs = jnp.where(mask, jnp.exp(scores - log_total[..., None]), 0.0)
        grad_probs = jnp.einsum(
            "sqhd,skhd->shqk", grad_att_heads, values, preferred_element_type=jnp.float32
        )
        grad_scores = (probs * (grad_probs - delta[..., None])).astype(jnp.bfloat16)
        grad_query = grad_query + jnp.einsum(
            "shqk,skhd->sqhd", grad_scores, keys, preferred_element_type=jnp.float32
        )
        grad_k = (
            jnp.einsum("shqk,sqhd->skhd", grad_scores, queries, preferred_element_type=jnp.float32)
            * scale
        )
        grad_v = jnp.einsum(
            "shqk,sqhd->skhd",
            probs.astype(jnp.bfloat16),
            grad_att_heads,
            preferred_element_type=jnp.float32,
        )
        joined = jnp.concatenate(
            [
                grad_k.reshape(seq_count, back_block, width),
                grad_v.reshape(seq_count, back_block, width),
            ],
            -1,
        )
        return (grad_query, lax.dynamic_update_slice_in_dim(grad_keys, joined, offset, 1))

    back_start = (
        jnp.zeros((seq_count, row_count, HEADS, head_dim), jnp.float32),
        jnp.zeros((seq_count, key_total, 2 * width), jnp.float32),
    )
    grad_query, grad_keys = lax.fori_loop(0, key_total // back_block, back_step, back_start)
    own_key_grads = lax.psum_scatter(
        grad_keys.astype(jnp.bfloat16), "ctx", scatter_dimension=1, tiled=True
    ).astype(jnp.float32)
    grad_merged = jnp.concatenate(
        [(grad_query * scale).reshape(seq_count, row_count, width), own_key_grads], -1
    ).astype(jnp.bfloat16)
    grad_one, grad_qkv_down, grad_qkv_up = project_back(
        grad_merged, normed_one, lowered_qkv, full_qkv, chosen[0], chosen[1]
    )
    input_grad = (grad_middle + norm_back(grad_one, scaled_one, inv_one, gain_one)).astype(
        jnp.bfloat16
    )
    picker_wide = picker.astype(jnp.float32)

    def spread(grad):
        return jnp.einsum("sa,srw->arw", picker_wide, grad).reshape(
            ADAPTERS * grad.shape[1], grad.shape[2]
        )

    term_a, term_b, term_c, term_d, term_e, term_f, term_g, term_h = [
        spread(grad)
        for grad in (
            grad_qkv_down,
            grad_qkv_up,
            grad_out_down,
            grad_out_up,
            grad_fc1_down,
            grad_fc1_up,
            grad_fc2_down,
            grad_fc2_up,
        )
    ]
    part_a, part_b, part_c, part_d, part_e, part_f, part_g, part_h = (
        lax.psum_scatter(
            term_a.astype(jnp.bfloat16), "ctx", scatter_dimension=1, tiled=True
        ).astype(jnp.float32),
        lax.psum_scatter(
            term_b.astype(jnp.bfloat16), "ctx", scatter_dimension=1, tiled=True
        ).astype(jnp.float32),
        lax.psum_scatter(
            term_c.astype(jnp.bfloat16), "ctx", scatter_dimension=1, tiled=True
        ).astype(jnp.float32),
        lax.psum_scatter(
            term_d.astype(jnp.bfloat16), "ctx", scatter_dimension=1, tiled=True
        ).astype(jnp.float32),
        lax.psum_scatter(
            term_e.astype(jnp.bfloat16), "ctx", scatter_dimension=1, tiled=True
        ).astype(jnp.float32),
        lax.psum_scatter(
            term_f.astype(jnp.bfloat16), "ctx", scatter_dimension=1, tiled=True
        ).astype(jnp.float32),
        lax.psum_scatter(
            term_g.astype(jnp.bfloat16), "ctx", scatter_dimension=1, tiled=True
        ).astype(jnp.float32),
        lax.psum_scatter(
            term_h.astype(jnp.bfloat16), "ctx", scatter_dimension=1, tiled=True
        ).astype(jnp.float32),
    )
    final_a, final_b, final_c, final_d, final_e, final_f, final_g, final_h = (
        lax.psum_scatter(part_a.astype(jnp.bfloat16), "dp", scatter_dimension=0, tiled=True).astype(
            jnp.float32
        ),
        lax.psum_scatter(part_b.astype(jnp.bfloat16), "dp", scatter_dimension=0, tiled=True).astype(
            jnp.float32
        ),
        lax.psum_scatter(part_c.astype(jnp.bfloat16), "dp", scatter_dimension=0, tiled=True).astype(
            jnp.float32
        ),
        lax.psum_scatter(part_d.astype(jnp.bfloat16), "dp", scatter_dimension=0, tiled=True).astype(
            jnp.float32
        ),
        lax.psum_scatter(part_e.astype(jnp.bfloat16), "dp", scatter_dimension=0, tiled=True).astype(
            jnp.float32
        ),
        lax.psum_scatter(part_f.astype(jnp.bfloat16), "dp", scatter_dimension=0, tiled=True).astype(
            jnp.float32
        ),
        lax.psum_scatter(part_g.astype(jnp.bfloat16), "dp", scatter_dimension=0, tiled=True).astype(
            jnp.float32
        ),
        lax.psum_scatter(part_h.astype(jnp.bfloat16), "dp", scatter_dimension=0, tiled=True).astype(
            jnp.float32
        ),
    )
    return (
        output,
        input_grad,
        final_a,
        final_b,
        final_c,
        final_d,
        final_e,
        final_f,
        final_g,
        final_h,
    )


def solution(mesh):
    return jax.shard_map(
        per_device,
        mesh=mesh,
        in_specs=(
            P("dp", "ctx", None),
            P("dp", None),
            P("dp"),
            P("ctx", "dp"),
            P("ctx", "dp"),
            P("ctx", "dp"),
            P("ctx", "dp"),
            P(),
            P(),
            P(),
            P(),
            P(),
            P(),
            P(),
            P(),
            P(),
            P(),
            P("dp", "ctx", None),
        ),
        out_specs=(
            P("dp", "ctx", None),
            P("dp", "ctx", None),
            P("dp", "ctx"),
            P("dp", "ctx"),
            P("dp", "ctx"),
            P("dp", "ctx"),
            P("dp", "ctx"),
            P("dp", "ctx"),
            P("dp", "ctx"),
            P("dp", "ctx"),
        ),
        check_vma=False,
    )
```

profile of v0, /device:TPU:0, one launch (start us, length us, event | category | flops | bytes accessed | tf_op | source)
XLA Modules:
  0.0 1883.6 jit_solution(2579130718959137755)
XLA Ops:
  8.0 33.1 %all-gather.23.cloned.1.call-done = bf16[8,408,272]{1,2,0:T(8,128)(2,1)} async-done(((bf16[1,408,272]{1,2,0:T(8,128)(2,1)}), bf16[8,408,272]{1,2,0:T(8,128)(2,1)}) %all-gather.23.cloned.1.call-update) | async-done | bytes 1775632 | tf_op jit(solution)/shard_map/all_gather | solution.py:62
  65.5 116.1 %all-gather.11.cloned.1.call-done = bf16[1088,3264]{1,0:T(8,128)(2,1)} async-done(((bf16[272,3264]{1,0:T(8,128)(2,1)}), bf16[1088,3264]{1,0:T(8,128)(2,1)}) %all-gather.11.cloned.1.call-update) | async-done | bytes 7102480 | tf_op jit(solution)/shard_map/all_gather | solution.py:68
  181.6 12.5 fusion.39
  202.0 13.2 all_gather.39
  259.4 294.8 %all-gather.13.cloned.1.call-done = bf16[2,2048,2176]{1,2,0:T(8,128)(2,1)} async-done(((bf16[2,512,2176]{1,2,0:T(8,128)(2,1)}), bf16[2,2048,2176]{1,2,0:T(8,128)(2,1)}) %all-gather.13.cloned.1.call-update) | async-done | bytes 17825808 | tf_op jit(solution)/shard_map/all_gather | solution.py:144
  554.2 220.1 %while.34 = (s32[]{:T(128)}, f32[2,17,512]{2,1,0:T(8,128)S(1)}, f32[2,17,512]{2,1,0:T(8,128)S(1)}, f32[2,512,17,64]{1,3,2,0:T(8,128)}, s32[2,2048]{1,0:T(2,128)}...) while((s32[]{:T(128)}, f32[2,17,512]{2,1,0:T(8,128)S(1)}, ...), condition=%wide.region_5.6_spmd.clone, body=%wide.region_2.5_spmd.clone.sunk | while | flops 2402327552 | bytes 135225584 | solution.py:158
  559.6 14.4 fusion.239
  574.0 15.4 fusion.241
  589.4 17.9 bitcast_add_fusion.4
  612.8 15.8 fusion.239
  628.6 15.4 fusion.241
  644.1 20.1 %bitcast_add_fusion.4 = f32[2,512,17,64]{1,3,2,0:T(8,128)} fusion(f32[2,512,17,64]{1,3,2,0:T(8,128)} %get-tuple-element.657, f32[2,512,17]{1,2,0:T(8,128)S(1)} %get-tuple-element.623, pred[]{:T(512)S(6)} %compare.6, bf16[2,512,17,64]{1,3,2,0:T(8,128)(2,1)} %bitcast.272, f32[2,17,512,512]{3,2,1,0:T(8,128)} %get-tuple-element.622, ...), kind=kOutput, calls=%fused_computation.9.clone.1 | convolution fusion | flops 1188757504 | bytes 47456256 | tf_op jit(solution)/shard_map/while/body/eval_jaxpr/shqk,skhd->sqhd/dot_general | solution.py:131
  669.7 14.4 fusion.239
  684.1 15.4 fusion.241
  699.5 19.9 %bitcast_add_fusion.4 = f32[2,512,17,64]{1,3,2,0:T(8,128)} fusion(f32[2,512,17,64]{1,3,2,0:T(8,128)} %get-tuple-element.657, f32[2,512,17]{1,2,0:T(8,128)S(1)} %get-tuple-element.623, pred[]{:T(512)S(6)} %compare.6, bf16[2,512,17,64]{1,3,2,0:T(8,128)(2,1)} %bitcast.272, f32[2,17,512,512]{3,2,1,0:T(8,128)} %get-tuple-element.622, ...), kind=kOutput, calls=%fused_computation.9.clone.1 | convolution fusion | flops 1188757504 | bytes 47456256 | tf_op jit(solution)/shard_map/while/body/eval_jaxpr/shqk,skhd->sqhd/dot_general | solution.py:131
  724.9 14.3 fusion.239
  739.2 15.3 fusion.241
  754.5 19.5 %bitcast_add_fusion.4 = f32[2,512,17,64]{1,3,2,0:T(8,128)} fusion(f32[2,512,17,64]{1,3,2,0:T(8,128)} %get-tuple-element.657, f32[2,512,17]{1,2,0:T(8,128)S(1)} %get-tuple-element.623, pred[]{:T(512)S(6)} %compare.6, bf16[2,512,17,64]{1,3,2,0:T(8,128)(2,1)} %bitcast.272, f32[2,17,512,512]{3,2,1,0:T(8,128)} %get-tuple-element.622, ...), kind=kOutput, calls=%fused_computation.9.clone.1 | convolution fusion | flops 1188757504 | bytes 47456256 | tf_op jit(solution)/shard_map/while/body/eval_jaxpr/shqk,skhd->sqhd/dot_general | solution.py:131
  801.5 28.2 %multiply_convert_fusion = (bf16[2,512,4352]{2,1,0:T(8,128)(2,1)}, f32[2,512,4352]{2,1,0:T(8,128)}) fusion(f32[2,512,4352]{2,1,0:T(8,128)} %fusion.97, bf16[2,512,1088]{1,2,0:T(8,128)(2,1)} %copy-done.17, bf16[1088,4352]{1,0:T(8,128)(2,1)} %all-gather.17.cloned.1.call-done), kind=kOutput, calls=%fused_computation.53 | convolution fusion | flops 9741795328 | bytes 56262656 | tf_op jit(solution)/shard_map/slw,wv->slv/dot_general | solution.py:36
  837.9 113.6 %all-gather.21.cloned.1.call-done = bf16[4352,1088]{1,0:T(8,128)(2,1)} async-done(((bf16[1088,1088]{1,0:T(8,128)(2,1)}), bf16[4352,1088]{1,0:T(8,128)(2,1)}) %all-gather.21.cloned.1.call-update) | async-done | bytes 9469968 | tf_op jit(solution)/shard_map/all_gather | solution.py:71
  951.5 26.8 %fusion.30 = bf16[2,512,4352]{2,1,0:T(8,128)(2,1)} fusion(f32[2,512,4352]{2,1,0:T(8,128)} %get-tuple-element.487, f32[2,512,4352]{2,1,0:T(8,128)} %fusion.93, bf16[2,512,1088]{1,2,0:T(8,128)(2,1)} %param.39, bf16[4352,1088]{1,0:T(8,128)(2,1)} %all-gather.21.cloned.1.call-done), kind=kOutput, calls=%fused_computation.52 | convolution fusion | flops 9790816256 | bytes 56262656 | tf_op jit(solution)/shard_map/slv,wv->slw/dot_general | solution.py:48
  989.3 17.1 fusion.159
  1042.4 10.1 reduce-scatter.56.cloned.1.call-done
  1062.4 18.9 %reduce-scatter.64.cloned.1.call-done = bf16[1088,128]{1,0:T(8,128)(2,1)} async-done(((bf16[4352,128]{1,0:T(8,128)(2,1)}), bf16[1088,128]{1,0:T(8,128)(2,1)}) %reduce-scatter.64.cloned.1.call-update) | async-done | bytes 278544
  1093.3 17.0 reduce-scatter.62.cloned.1.call-done
  1118.7 338.8 %while.35 = (s32[]{:T(128)}, f32[2,512,17,64]{1,3,2,0:T(8,128)}, bf16[2,2048,2176]{1,2,0:T(8,128)(2,1)}, bf16[2,2048,2176]{1,2,0:T(8,128)(2,1)}, s32[2,2048]{1,0...) while((s32[]{:T(128)}, f32[2,512,17,64]{1,3,2,0:T(8,128)}, ...), condition=%wide.region_12.13_spmd.clone, body=%wide.region_11.12_spmd.clone.sunk | while | flops 5808063488 | bytes 236294480 | solution.py:247
  1125.1 15.6 fusion.253
  1140.7 16.6 fusion.255
  1157.3 22.0 %fusion.254 = bf16[2,17,512,512]{2,3,1,0:T(8,128)(2,1)} fusion(f32[2,17,512,512]{3,2,1,0:T(8,128)} %fusion.253, bf16[2,512,17,64]{1,3,2,0:T(8,128)(2,1)} %bitcast.274, bf16[2,512,17,64]{1,3,2,0:T(8,128)(2,1)} %get-tuple-element.722, f32[2,17,512]{2,1,0:T(8,128)S(1)} %get-tuple-element.723, f32[2,17,512]{2,1,0:T(8,128)S(1)} %get-tuple-element.721, ...), kind=kOutput, calls=%fused_computation.27.clone.1 | convolution fusion | flops 1194328064 | bytes 58597376 | tf_op jit(solution)/shard_map/while/body/eval_jaxpr/sqhd,skhd->shqk/dot_general | solution.py:217
  1179.3 11.0 bitcast_add_fusion.5
  1208.8 15.6 fusion.253
  1224.4 16.7 fusion.255
  1241.0 22.0 %fusion.254 = bf16[2,17,512,512]{2,3,1,0:T(8,128)(2,1)} fusion(f32[2,17,512,512]{3,2,1,0:T(8,128)} %fusion.253, bf16[2,512,17,64]{1,3,2,0:T(8,128)(2,1)} %bitcast.274, bf16[2,512,17,64]{1,3,2,0:T(8,128)(2,1)} %get-tuple-element.722, f32[2,17,512]{2,1,0:T(8,128)S(1)} %get-tuple-element.723, f32[2,17,512]{2,1,0:T(8,128)S(1)} %get-tuple-element.721, ...), kind=kOutput, calls=%fused_computation.27.clone.1 | convolution fusion | flops 1194328064 | bytes 58597376 | tf_op jit(solution)/shard_map/while/body/eval_jaxpr/sqhd,skhd->shqk/dot_general | solution.py:217
  1263.0 12.3 bitcast_add_fusion.5
  1293.8 15.6 fusion.253
  1309.4 16.6 fusion.255
  1326.0 22.0 %fusion.254 = bf16[2,17,512,512]{2,3,1,0:T(8,128)(2,1)} fusion(f32[2,17,512,512]{3,2,1,0:T(8,128)} %fusion.253, bf16[2,512,17,64]{1,3,2,0:T(8,128)(2,1)} %bitcast.274, bf16[2,512,17,64]{1,3,2,0:T(8,128)(2,1)} %get-tuple-element.722, f32[2,17,512]{2,1,0:T(8,128)S(1)} %get-tuple-element.723, f32[2,17,512]{2,1,0:T(8,128)S(1)} %get-tuple-element.721, ...), kind=kOutput, calls=%fused_computation.27.clone.1 | convolution fusion | flops 1194328064 | bytes 58597376 | tf_op jit(solution)/shard_map/while/body/eval_jaxpr/sqhd,skhd->shqk/dot_general | solution.py:217
  1348.0 12.2 bitcast_add_fusion.5
  1378.7 15.5 fusion.253
  1394.2 16.5 fusion.255
  1410.8 22.0 %fusion.254 = bf16[2,17,512,512]{2,3,1,0:T(8,128)(2,1)} fusion(f32[2,17,512,512]{3,2,1,0:T(8,128)} %fusion.253, bf16[2,512,17,64]{1,3,2,0:T(8,128)(2,1)} %bitcast.274, bf16[2,512,17,64]{1,3,2,0:T(8,128)(2,1)} %get-tuple-element.722, f32[2,17,512]{2,1,0:T(8,128)S(1)} %get-tuple-element.723, f32[2,17,512]{2,1,0:T(8,128)S(1)} %get-tuple-element.721, ...), kind=kOutput, calls=%fused_computation.27.clone.1 | convolution fusion | flops 1194328064 | bytes 58597376 | tf_op jit(solution)/shard_map/while/body/eval_jaxpr/sqhd,skhd->shqk/dot_general | solution.py:217
  1432.7 12.2 bitcast_add_fusion.5
  1462.7 18.8 fusion.71
  1489.6 264.0 %reduce-scatter.34.cloned.1.call-done = bf16[2,512,2176]{1,2,0:T(8,128)(2,1)} async-done(((bf16[2,2048,2176]{1,2,0:T(8,128)(2,1)}), bf16[2,512,2176]{1,2,0:T(8,128)(2,1)}) %reduce-scatter.34.cloned.1.call-update) | async-done | bytes 4456464 | tf_op jit(solution)/shard_map/reduce_scatter | solution.py:248
  1768.4 15.0 fusion.158
  1785.2 20.7 %reduce-scatter.54.cloned.1.call-done = bf16[816,128]{1,0:T(8,128)(2,1)} async-done(((bf16[3264,128]{1,0:T(8,128)(2,1)}), bf16[816,128]{1,0:T(8,128)(2,1)}) %reduce-scatter.54.cloned.1.call-update) | async-done | bytes 208912
  1814.2 26.2 %reduce-scatter.36.cloned.1.call-done = bf16[16,272]{1,0:T(8,128)(2,1)} async-done(((bf16[128,272]{1,0:T(8,128)(2,1)}), bf16[16,272]{1,0:T(8,128)(2,1)}) %reduce-scatter.36.cloned.1.call-update) | async-done | bytes 8720 | tf_op jit(solution)/shard_map/reduce_scatter | solution.py:307
  1841.7 33.8 %reduce-scatter.38.cloned.1.call-done = bf16[16,816]{1,0:T(8,128)(2,1)} async-done(((bf16[128,816]{1,0:T(8,128)(2,1)}), bf16[16,816]{1,0:T(8,128)(2,1)}) %reduce-scatter.38.cloned.1.call-update) | async-done | bytes 26128 | tf_op jit(solution)/shard_map/reduce_scatter | solution.py:310
  (370 shorter events, 325.3 us)
Async XLA Ops:
  7.2 234.6 %copy-start = (bf16[128,4352]{1,0:T(8,128)(2,1)S(1)}, bf16[128,4352]{1,0:T(8,128)(2,1)}, u32[]{:S(2)}) copy-start(bf16[128,4352]{1,0:T(8,128)(2,1)} %param.36) | copy-start | bytes 3342340
  7.2 33.9 %all-gather.23.cloned.1.call-start = ((), (), s32[]{:S(2)}) async-start(), calls=%async_computation.32 | async-start | bytes 2506752 | tf_op jit(solution)/shard_map/all_gather | solution.py:62
  7.9 44.3 %copy-start.8 = (bf16[2,512,1088]{1,2,0:T(8,128)(2,1)S(1)}, bf16[2,512,1088]{1,2,0:T(8,128)(2,1)}, u32[]{:S(2)}) copy-start(bf16[2,512,1088]{1,2,0:T(8,128)(2,1)} %param.22) | copy-start | bytes 6684676
  7.9 173.6 %all-gather.11.cloned.1.call-start = ((), (), s32[]{:S(2)}) async-start(), calls=%async_computation.17 | async-start | bytes 9052160 | tf_op jit(solution)/shard_map/all_gather | solution.py:68
  50.5 8.0 copy-start.43
  50.5 166.5 %all-gather.25.cloned.1.call-start = ((), (), s32[]{:S(2)}) async-start(), calls=%async_computation.33 | async-start | bytes 3133440 | tf_op jit(solution)/shard_map/all_gather | solution.py:64
  51.3 202.7 %all-gather.19.cloned.1.call-start = ((), (), s32[]{:S(2)}) async-start(), calls=%async_computation.21 | async-start | bytes 2820096 | tf_op jit(solution)/shard_map/all_gather | solution.py:65
  51.8 502.4 %all-gather.13.cloned.1.call-start = ((), (), s32[]{:S(2)}) async-start(), calls=%async_computation.18 | async-start | bytes 22282240 | tf_op jit(solution)/shard_map/all_gather | solution.py:144
  61.5 132.5 %copy-start.26 = (bf16[2,16,3264]{2,0,1:T(2,128)(2,1)}, bf16[2,16,3264]{2,0,1:T(2,128)(2,1)S(1)}, u32[]{:S(2)}) copy-start(bf16[2,16,3264]{2,0,1:T(2,128)(2,1)S(1)} %convolution_convert_fusion.5) | copy-start | bytes 626692
  65.5 128.6 %copy-start.47 = (bf16[2,512,16]{1,2,0:T(8,128)(2,1)}, bf16[2,512,16]{1,2,0:T(8,128)(2,1)S(1)}, u32[]{:S(2)}) copy-start(bf16[2,512,16]{1,2,0:T(8,128)(2,1)S(1)} %convolution_convert_fusion.21) | copy-start | bytes 98308
  201.1 580.5 %all-gather.15.cloned.1.call-start = ((), (), s32[]{:S(2)}) async-start(), calls=%async_computation.19 | async-start | bytes 3133440 | tf_op jit(solution)/shard_map/all_gather | solution.py:69
  216.3 585.2 %all-gather.17.cloned.1.call-start = ((), (), s32[]{:S(2)}) async-start(), calls=%async_computation.20 | async-start | bytes 11837440 | tf_op jit(solution)/shard_map/all_gather | solution.py:70
  220.9 14.0 copy-start.44
  226.6 18.4 copy-start.19
  226.6 724.9 %all-gather.21.cloned.1.call-start = ((), (), s32[]{:S(2)}) async-start(), calls=%async_computation.22 | async-start | bytes 12533760 | tf_op jit(solution)/shard_map/all_gather | solution.py:71
  244.9 9.0 copy-start.23
  245.3 8.6 copy-start.28
  259.2 295.1 %slice-start = ((bf16[2,512,3264]{1,2,0:T(8,128)(2,1)}), bf16[2,512,1088]{1,2,0:T(8,128)(2,1)S(1)}, s32[]{:S(2)}) async-start(bf16[2,512,3264]{1,2,0:T(8,128)(2,1)} %copy-done.2), calls=%async_computation.42 | async-start | bytes 4456448 | tf_op jit(solution)/shard_map/slice | solution.py:118
  259.2 778.0 %reduce-scatter.66.cloned.1.call-start = ((), (), s32[]{:S(2)}) async-start(), calls=%async_computation.41 | async-start | bytes 348160
  801.5 28.2 %copy-start.24 = (bf16[2,16,4352]{2,0,1:T(2,128)(2,1)S(1)}, bf16[2,16,4352]{2,0,1:T(2,128)(2,1)}, u32[]{:S(2)}) copy-start(bf16[2,16,4352]{2,0,1:T(2,128)(2,1)} %copy-done.23) | copy-start | bytes 835588
  829.7 6.8 copy-start.45
  835.9 142.4 %copy-start.39 = (bf16[2,512,16]{1,2,0:T(8,128)(2,1)}, bf16[2,512,16]{1,2,0:T(8,128)(2,1)S(1)}, u32[]{:S(2)}) copy-start(bf16[2,512,16]{1,2,0:T(8,128)(2,1)S(1)} %convolution_convert_fusion.17) | copy-start | bytes 98308
  837.9 201.1 %reduce-scatter.60.cloned.1.call-start = ((), (), s32[]{:S(2)}) async-start(), calls=%async_computation.38 | async-start | bytes 348160
  989.2 51.5 %reduce-scatter.58.cloned.1.call-start = ((), (), s32[]{:S(2)}) async-start(), calls=%async_computation.37 | async-start | bytes 348160
  989.3 17.1 copy-start.21
  1014.0 38.5 %reduce-scatter.56.cloned.1.call-start = ((), (), s32[]{:S(2)}) async-start(), calls=%async_computation.36 | async-start | bytes 348160
  1019.1 62.2 %reduce-scatter.64.cloned.1.call-start = ((), (), s32[]{:S(2)}) async-start(), calls=%async_computation.40 | async-start | bytes 1392640
  1028.1 82.3 %reduce-scatter.62.cloned.1.call-start = ((), (), s32[]{:S(2)}) async-start(), calls=%async_computation.39 | async-start | bytes 1392640
  1037.1 444.3 %reduce-scatter.50.cloned.1.call-start = ((), (), s32[]{:S(2)}) async-start(), calls=%async_computation.31 | async-start | bytes 110592 | tf_op jit(solution)/shard_map/reduce_scatter | solution.py:328
  1038.9 443.9 %reduce-scatter.44.cloned.1.call-start = ((), (), s32[]{:S(2)}) async-start(), calls=%async_computation.28 | async-start | bytes 110592 | tf_op jit(solution)/shard_map/reduce_scatter | solution.py:319
  1040.6 443.5 %reduce-scatter.42.cloned.1.call-start = ((), (), s32[]{:S(2)}) async-start(), calls=%async_computation.27 | async-start | bytes 110592 | tf_op jit(solution)/shard_map/reduce_scatter | solution.py:316
  1042.3 443.1 %reduce-scatter.40.cloned.1.call-start = ((), (), s32[]{:S(2)}) async-start(), calls=%async_computation.26 | async-start | bytes 110592 | tf_op jit(solution)/shard_map/reduce_scatter | solution.py:313
  1054.2 29.0 %copy-start.32 = (bf16[2,16,1088]{2,0,1:T(2,128)(2,1)S(1)}, bf16[2,16,1088]{2,0,1:T(2,128)(2,1)}, u32[]{:S(2)}) copy-start(bf16[2,16,1088]{2,0,1:T(2,128)(2,1)} %convolution_convert_fusion.14) | copy-start | bytes 208900
  1054.2 29.0 %copy-start.42 = (bf16[2,512,16]{1,2,0:T(8,128)(2,1)S(1)}, bf16[2,512,16]{1,2,0:T(8,128)(2,1)}, u32[]{:S(2)}) copy-start(bf16[2,512,16]{1,2,0:T(8,128)(2,1)} %copy-done.41) | copy-start | bytes 98308
  1054.2 432.6 %reduce-scatter.48.cloned.1.call-start = ((), (), s32[]{:S(2)}) async-start(), calls=%async_computation.30 | async-start | bytes 331776 | tf_op jit(solution)/shard_map/reduce_scatter | solution.py:325
  1083.1 405.1 %reduce-scatter.46.cloned.1.call-start = ((), (), s32[]{:S(2)}) async-start(), calls=%async_computation.29 | async-start | bytes 331776 | tf_op jit(solution)/shard_map/reduce_scatter | solution.py:322
  1112.2 641.3 %reduce-scatter.34.cloned.1.call-start = ((), (), s32[]{:S(2)}) async-start(), calls=%async_computation.23 | async-start | bytes 22282240 | tf_op jit(solution)/shard_map/reduce_scatter | solution.py:248
  1190.3 10.0 copy-start.11
  1275.3 10.0 copy-start.11
  1360.2 9.9 copy-start.11
  1445.0 9.9 copy-start.11
  1457.6 325.9 %reduce-scatter.52.cloned.1.call-start = ((), (), s32[]{:S(2)}) async-start(), calls=%async_computation.34 | async-start | bytes 348160
  1462.7 297.1 %copy-start.25 = (bf16[2,512,17,64]{1,3,2,0:T(8,128)(2,1)}, bf16[2,512,17,64]{1,3,2,0:T(8,128)(2,1)S(1)}, u32[]{:S(2)}) copy-start(bf16[2,512,17,64]{1,3,2,0:T(8,128)(2,1)S(1)} %multiply_convert_fusion.1) | copy-start | bytes 6684676
  1462.7 290.9 %copy-start.27 = (bf16[2,16,3264]{2,0,1:T(2,128)(2,1)S(1)}, bf16[2,16,3264]{2,0,1:T(2,128)(2,1)}, u32[]{:S(2)}) copy-start(bf16[2,16,3264]{2,0,1:T(2,128)(2,1)} %copy-done.26) | copy-start | bytes 626692
  1759.7 46.2 %reduce-scatter.54.cloned.1.call-start = ((), (), s32[]{:S(2)}) async-start(), calls=%async_computation.35 | async-start | bytes 1044480
  1768.3 72.1 %reduce-scatter.36.cloned.1.call-start = ((), (), s32[]{:S(2)}) async-start(), calls=%async_computation.24 | async-start | bytes 110592 | tf_op jit(solution)/shard_map/reduce_scatter | solution.py:307
  1785.1 90.4 %reduce-scatter.38.cloned.1.call-start = ((), (), s32[]{:S(2)}) async-start(), calls=%async_computation.25 | async-start | bytes 258048 | tf_op jit(solution)/shard_map/reduce_scatter | solution.py:310
  1807.8 69.1 %copy-start.1 = (bf16[128,4352]{1,0:T(8,128)(2,1)S(1)}, bf16[128,4352]{1,0:T(8,128)(2,1)}, u32[]{:S(2)}) copy-start(bf16[128,4352]{1,0:T(8,128)(2,1)} %param.36) | copy-start | bytes 3342340
  (44 other events, 126.4 us)
Sparse Core Ops, SparseCore 0:
  9.9 31.1 all-gather.22
  50.7 130.8 all-gather.10
  183.5 31.4 all-gather.24
  216.7 30.4 all-gather.18
  248.7 305.5 all-gather.12
  555.7 51.8 all-gather.14
  609.1 166.0 all-gather.16
  776.8 174.6 all-gather.20
  953.8 18.0 reduce-scatter.65
  989.3 18.0 reduce-scatter.59
  1014.2 18.0 reduce-scatter.57
  1034.4 18.1 reduce-scatter.55
  1054.8 26.3 reduce-scatter.63
  1083.5 26.8 reduce-scatter.61
  1113.2 31.0 reduce-scatter.49
  1147.2 32.4 reduce-scatter.43
  1182.6 32.4 reduce-scatter.41
  1217.9 32.4 reduce-scatter.39
  1253.5 32.8 reduce-scatter.47
  1289.3 32.9 reduce-scatter.45
  1457.7 295.8 reduce-scatter.33
  1759.8 20.7 reduce-scatter.51
  1783.6 22.2 reduce-scatter.53
  1808.8 31.5 reduce-scatter.35
  1843.5 31.9 reduce-scatter.37
where the time goes:
time: 1890 us; the launch traced here: 1880 us
  waiting for transfers between devices  951 us (50%)
  matrix products  663 us (35%)
  local copies, waits for them, and re-layouts  129 us (7%)
  other arithmetic  109 us (6%)
    all_gather x1, waiting for transfers between devices, per_device(): piece = lax.all_gather(key_vals, 'ctx', axis=1, tiled=True)  295 us
    reduce_scatter x1, waiting for transfers between devices, per_device(): lax.psum_scatter(grad_keys.astype(jnp.bfloat16), 'ctx', scatter_dimension...  264 us
    all_gather x1, waiting for transfers between devices, gather_weights(): lax.all_gather(wide_qkv, 'ctx', axis=0, tiled=True)  116 us
    all_gather x1, waiting for transfers between devices, gather_weights(): lax.all_gather(wide_fc2, 'ctx', axis=0, tiled=True)  114 us
    dot_general x4, matrix products, back_step(): jnp.einsum('sqhd,skhd->shqk', grad_att_heads, values, preferred_element_t...  88 us
    dot_general x4, matrix products, attend(): jnp.einsum('shqk,skhd->sqhd', expo_term.astype(jnp.bfloat16), values, pre...  77.4 us
    unnamed x33, waiting for transfers between devices  69.1 us
    dot_general x4, matrix products, project_back(): jnp.einsum('slv,wv->slw', grad_low, weight, preferred_element_type=jnp.fl...  67.1 us
  transfers between devices with their start and end apart: 25, of which 11 were waited for; matrix products, arithmetic and copies ran while one was open for 46% of the time, Pallas kernels for 0%

commit v1 on v0

--- a/solution.py
+++ b/solution.py
@@ -7,6 +7,21 @@
 ADAPTERS = 8
 eps = 1e-05
 neg_big = -1e30
+
+
+def set_the_boxes(target):
+    num = lax.psum(1, "ctx")
+    found = [target]
+    ix = 1
+    while ix < num:
+        item_now = lax.ppermute(
+            found[ix - 1], "ctx", [(dev_i, (dev_i - 1) % num) for dev_i in range(num)]
+        )
+        found.append(item_now)
+        ix = ix + 1
+    all_rows = jnp.concatenate(found, axis=0)
+    mixed_arr = lax.axis_index("ctx")
+    return jnp.roll(all_rows, mixed_arr * target.shape[0], axis=0)
 
 
 def norm_rows(vector, gain):
@@ -68,7 +83,7 @@
         lax.all_gather(wide_qkv, "ctx", axis=0, tiled=True),
         lax.all_gather(wide_out, "ctx", axis=0, tiled=True),
         lax.all_gather(wide_fc1, "ctx", axis=0, tiled=True),
-        lax.all_gather(wide_fc2, "ctx", axis=0, tiled=True),
+        set_the_boxes(wide_fc2),
     )
 
 

time: 1890 us -> 1890 us (level)
    ppermute x0 -> x3, waiting for transfers between devices: none -> 349 us  [set_the_boxes(): lax.ppermute(found[ix - 1], 'ctx', [(dev_i, (dev_i - 1) % num) for dev_i...]
    all_gather x1, waiting for transfers between devices: 295 us -> 28.2 us  [per_device(): piece = lax.all_gather(key_vals, 'ctx', axis=1, tiled=True)]
    all_gather x1 -> x0, waiting for transfers between devices: 114 us -> none  [gather_weights(): lax.all_gather(wide_fc2, 'ctx', axis=0, tiled=True)]
    unnamed x33 -> x32, waiting for transfers between devices: 69.1 us -> 76.7 us
    unnamed x132 -> x134, local copies, waits for them, and re-layouts: 61.5 us -> 56.9 us
  transfers between devices with their start and end apart: 25 -> 27, of which waited for: 11 -> 14; matrix products, arithmetic and copies ran while one was open for 46% -> 45% of each run, Pallas kernels for 0% -> 0%
where the time goes in v1:
time: 1890 us; the launch traced here: 1880 us
  waiting for transfers between devices  936 us (50%)
  matrix products  663 us (35%)
  local copies, waits for them, and re-layouts  133 us (7%)
  other arithmetic  110 us (6%)
    ppermute x3, waiting for transfers between devices, set_the_boxes(): lax.ppermute(found[ix - 1], 'ctx', [(dev_i, (dev_i - 1) % num) for dev_i...  349 us
    reduce_scatter x1, waiting for transfers between devices, per_device(): lax.psum_scatter(grad_keys.astype(jnp.bfloat16), 'ctx', scatter_dimension...  263 us
    all_gather x1, waiting for transfers between devices, gather_weights(): lax.all_gather(wide_qkv, 'ctx', axis=0, tiled=True)  116 us
    dot_general x4, matrix products, back_step(): jnp.einsum('sqhd,skhd->shqk', grad_att_heads, values, preferred_element_t...  88.1 us
    dot_general x4, matrix products, attend(): jnp.einsum('shqk,skhd->sqhd', expo_term.astype(jnp.bfloat16), values, pre...  77.4 us
    unnamed x32, waiting for transfers between devices  76.7 us
    dot_general x4, matrix products, project_back(): jnp.einsum('slv,wv->slw', grad_low, weight, preferred_element_type=jnp.fl...  74.9 us
    dot_general x4, matrix products, back_step(): jnp.einsum('shqk,sqhd->skhd', probs.astype(jnp.bfloat16), grad_att_heads,...  66.6 us
  transfers between devices with their start and end apart: 27, of which 14 were waited for; matrix products, arithmetic and copies ran while one was open for 45% of the time, Pallas kernels for 0%

profile of v1, /device:TPU:0, one launch (start us, length us, event | category | flops | bytes accessed | tf_op | source)
XLA Modules:
  0.0 1879.1 jit_solution(18049242421606448883)
XLA Ops:
  8.0 33.1 %all-gather.20.cloned.1.call-done = bf16[8,408,272]{1,2,0:T(8,128)(2,1)} async-done(((bf16[1,408,272]{1,2,0:T(8,128)(2,1)}), bf16[8,408,272]{1,2,0:T(8,128)(2,1)}) %all-gather.20.cloned.1.call-update) | async-done | bytes 1775632 | tf_op jit(solution)/shard_map/all_gather | solution.py:77
  65.7 115.9 %all-gather.10.cloned.1.call-done = bf16[1088,3264]{1,0:T(8,128)(2,1)} async-done(((bf16[272,3264]{1,0:T(8,128)(2,1)}), bf16[1088,3264]{1,0:T(8,128)(2,1)}) %all-gather.10.cloned.1.call-update) | async-done | bytes 7102480 | tf_op jit(solution)/shard_map/all_gather | solution.py:83
  181.6 12.5 fusion.38
  214.7 63.7 %collective-permute-done = bf16[1088,1088]{0,1:T(8,128)(2,1)} collective-permute-done((bf16[1088,1088]{0,1:T(8,128)(2,1)}, bf16[1088,1088]{0,1:T(8,128)(2,1)}, u32[]{:S(2)}, u32[]{:S(2)}) %collective-permute-start) | collective-permute-done | bytes 2367520 | tf_op jit(solution)/shard_map/ppermute | solution.py:17
  304.5 147.5 %collective-permute-done.1 = bf16[1088,1088]{0,1:T(8,128)(2,1)} collective-permute-done((bf16[1088,1088]{0,1:T(8,128)(2,1)}, bf16[1088,1088]{0,1:T(8,128)(2,1)}, u32[]{:S(2)}, u32[]{:S(2)}) %collective-permute-start.1) | collective-permute-done | bytes 2367520 | tf_op jit(solution)/shard_map/ppermute | solution.py:17
  480.9 138.2 %collective-permute-done.2 = bf16[1088,1088]{0,1:T(8,128)(2,1)} collective-permute-done((bf16[1088,1088]{0,1:T(8,128)(2,1)}, bf16[1088,1088]{0,1:T(8,128)(2,1)}, u32[]{:S(2)}, u32[]{:S(2)}) %collective-permute-start.2) | collective-permute-done | bytes 2367520 | tf_op jit(solution)/shard_map/ppermute | solution.py:17
  619.1 16.1 concatenate.18
  635.2 28.2 %all-gather.12.cloned.1.call-done = bf16[2,2048,2176]{1,2,0:T(8,128)(2,1)} async-done(((bf16[2,512,2176]{1,2,0:T(8,128)(2,1)}), bf16[2,2048,2176]{1,2,0:T(8,128)(2,1)}) %all-gather.12.cloned.1.call-update) | async-done | bytes 17825808 | tf_op jit(solution)/shard_map/all_gather | solution.py:159
  663.4 221.2 %while.34 = (s32[]{:T(128)}, f32[2,17,512]{2,1,0:T(8,128)S(1)}, f32[2,17,512]{2,1,0:T(8,128)S(1)}, f32[2,512,17,64]{1,3,2,0:T(8,128)}, s32[2,2048]{1,0:T(2,128)}...) while((s32[]{:T(128)}, f32[2,17,512]{2,1,0:T(8,128)S(1)}, ...), condition=%wide.region_5.6_spmd.clone, body=%wide.region_2.5_spmd.clone.sunk | while | flops 2402327552 | bytes 135225584 | solution.py:173
  668.8 14.8 fusion.237
  683.6 15.4 fusion.239
  699.0 17.9 bitcast_add_fusion.5
  722.4 16.3 fusion.237
  738.7 15.4 fusion.239
  754.1 20.0 %bitcast_add_fusion.5 = f32[2,512,17,64]{1,3,2,0:T(8,128)} fusion(f32[2,512,17,64]{1,3,2,0:T(8,128)} %get-tuple-element.658, f32[2,512,17]{1,2,0:T(8,128)S(1)} %get-tuple-element.624, pred[]{:T(512)S(6)} %compare.6, bf16[2,512,17,64]{1,3,2,0:T(8,128)(2,1)} %bitcast.268, f32[2,17,512,512]{3,2,1,0:T(8,128)} %get-tuple-element.623, ...), kind=kOutput, calls=%fused_computation.9.clone.1 | convolution fusion | flops 1188757504 | bytes 47456256 | tf_op jit(solution)/shard_map/while/body/eval_jaxpr/shqk,skhd->sqhd/dot_general | solution.py:146
  779.6 14.5 fusion.237
  794.2 15.4 fusion.239
  809.5 20.0 %bitcast_add_fusion.5 = f32[2,512,17,64]{1,3,2,0:T(8,128)} fusion(f32[2,512,17,64]{1,3,2,0:T(8,128)} %get-tuple-element.658, f32[2,512,17]{1,2,0:T(8,128)S(1)} %get-tuple-element.624, pred[]{:T(512)S(6)} %compare.6, bf16[2,512,17,64]{1,3,2,0:T(8,128)(2,1)} %bitcast.268, f32[2,17,512,512]{3,2,1,0:T(8,128)} %get-tuple-element.623, ...), kind=kOutput, calls=%fused_computation.9.clone.1 | convolution fusion | flops 1188757504 | bytes 47456256 | tf_op jit(solution)/shard_map/while/body/eval_jaxpr/shqk,skhd->sqhd/dot_general | solution.py:146
  835.0 14.3 fusion.237
  849.3 15.3 fusion.239
  864.6 19.5 %bitcast_add_fusion.5 = f32[2,512,17,64]{1,3,2,0:T(8,128)} fusion(f32[2,512,17,64]{1,3,2,0:T(8,128)} %get-tuple-element.658, f32[2,512,17]{1,2,0:T(8,128)S(1)} %get-tuple-element.624, pred[]{:T(512)S(6)} %compare.6, bf16[2,512,17,64]{1,3,2,0:T(8,128)(2,1)} %bitcast.268, f32[2,17,512,512]{3,2,1,0:T(8,128)} %get-tuple-element.623, ...), kind=kOutput, calls=%fused_computation.9.clone.1 | convolution fusion | flops 1188757504 | bytes 47456256 | tf_op jit(solution)/shard_map/while/body/eval_jaxpr/shqk,skhd->sqhd/dot_general | solution.py:146
  910.5 25.4 %multiply_convert_fusion = (bf16[2,512,4352]{2,1,0:T(8,128)(2,1)}, f32[2,512,4352]{2,1,0:T(8,128)}) fusion(f32[2,512,4352]{2,1,0:T(8,128)} %fusion.91, bf16[2,512,1088]{1,2,0:T(8,128)(2,1)S(1)} %multiply_convert_fusion.2, bf16[1088,4352]{1,0:T(8,128)(2,1)} %all-gather.16.cloned.1.call-done), kind=kOutput, calls=%fused_computation.56 | convolution fusion | flops 9741795328 | bytes 56262656 | tf_op jit(solution)/shard_map/slw,wv->slv/dot_general | solution.py:51
  944.0 34.3 %fusion.30 = bf16[2,512,4352]{2,1,0:T(8,128)(2,1)} fusion(f32[2,512,4352]{2,1,0:T(8,128)} %get-tuple-element.488, f32[2,512,4352]{2,1,0:T(8,128)} %fusion.87, bf16[2,512,1088]{1,2,0:T(8,128)(2,1)} %param.41, s32[]{:T(128)S(6)} %select_n.59, bf16[4352,1088]{0,1:T(8,128)(2,1)} %concatenate.18), kind=kOutput, calls=%fused_computation.54 | convolution fusion | flops 9809756160 | bytes 56262660 | tf_op jit(solution)/shard_map/slv,wv->slw/dot_general | solution.py:63
  989.2 17.3 fusion.157
  1038.3 17.2 reduce-scatter.56.cloned.1.call-done
  1065.4 19.3 %reduce-scatter.64.cloned.1.call-done = bf16[1088,128]{1,0:T(8,128)(2,1)} async-done(((bf16[4352,128]{1,0:T(8,128)(2,1)}), bf16[1088,128]{1,0:T(8,128)(2,1)}) %reduce-scatter.64.cloned.1.call-update) | async-done | bytes 278544
  1096.8 17.2 reduce-scatter.62.cloned.1.call-done
  1122.4 330.3 %while.35 = (s32[]{:T(128)}, f32[2,512,17,64]{1,3,2,0:T(8,128)}, bf16[2,2048,2176]{1,2,0:T(8,128)(2,1)}, bf16[2,2048,2176]{1,2,0:T(8,128)(2,1)}, s32[2,2048]{1,0...) while((s32[]{:T(128)}, f32[2,512,17,64]{1,3,2,0:T(8,128)}, ...), condition=%wide.region_12.14_spmd.clone, body=%wide.region_11.13_spmd.clone.sunk | while | flops 5808063488 | bytes 236294480 | solution.py:262
  1128.3 14.0 fusion.251
  1142.3 16.6 fusion.253
  1158.9 22.1 %fusion.252 = bf16[2,17,512,512]{2,3,1,0:T(8,128)(2,1)} fusion(f32[2,17,512,512]{3,2,1,0:T(8,128)} %fusion.251, bf16[2,512,17,64]{1,3,2,0:T(8,128)(2,1)} %bitcast.270, bf16[2,512,17,64]{1,3,2,0:T(8,128)(2,1)} %get-tuple-element.723, f32[2,17,512]{2,1,0:T(8,128)S(1)} %get-tuple-element.724, f32[2,17,512]{2,1,0:T(8,128)S(1)} %get-tuple-element.722, ...), kind=kOutput, calls=%fused_computation.27.clone.1 | convolution fusion | flops 1194328064 | bytes 58597376 | tf_op jit(solution)/shard_map/while/body/eval_jaxpr/sqhd,skhd->shqk/dot_general | solution.py:232
  1209.7 14.0 fusion.251
  1223.7 16.7 fusion.253
  1240.4 22.0 %fusion.252 = bf16[2,17,512,512]{2,3,1,0:T(8,128)(2,1)} fusion(f32[2,17,512,512]{3,2,1,0:T(8,128)} %fusion.251, bf16[2,512,17,64]{1,3,2,0:T(8,128)(2,1)} %bitcast.270, bf16[2,512,17,64]{1,3,2,0:T(8,128)(2,1)} %get-tuple-element.723, f32[2,17,512]{2,1,0:T(8,128)S(1)} %get-tuple-element.724, f32[2,17,512]{2,1,0:T(8,128)S(1)} %get-tuple-element.722, ...), kind=kOutput, calls=%fused_computation.27.clone.1 | convolution fusion | flops 1194328064 | bytes 58597376 | tf_op jit(solution)/shard_map/while/body/eval_jaxpr/sqhd,skhd->shqk/dot_general | solution.py:232
  1262.5 12.6 bitcast_add_fusion.6
  1292.8 14.2 fusion.251
  1306.9 16.7 fusion.253
  1323.6 22.0 %fusion.252 = bf16[2,17,512,512]{2,3,1,0:T(8,128)(2,1)} fusion(f32[2,17,512,512]{3,2,1,0:T(8,128)} %fusion.251, bf16[2,512,17,64]{1,3,2,0:T(8,128)(2,1)} %bitcast.270, bf16[2,512,17,64]{1,3,2,0:T(8,128)(2,1)} %get-tuple-element.723, f32[2,17,512]{2,1,0:T(8,128)S(1)} %get-tuple-element.724, f32[2,17,512]{2,1,0:T(8,128)S(1)} %get-tuple-element.722, ...), kind=kOutput, calls=%fused_computation.27.clone.1 | convolution fusion | flops 1194328064 | bytes 58597376 | tf_op jit(solution)/shard_map/while/body/eval_jaxpr/sqhd,skhd->shqk/dot_general | solution.py:232
  1345.6 12.4 bitcast_add_fusion.6
  1375.6 14.0 fusion.251
  1389.5 16.6 fusion.253
  1406.1 22.0 %fusion.252 = bf16[2,17,512,512]{2,3,1,0:T(8,128)(2,1)} fusion(f32[2,17,512,512]{3,2,1,0:T(8,128)} %fusion.251, bf16[2,512,17,64]{1,3,2,0:T(8,128)(2,1)} %bitcast.270, bf16[2,512,17,64]{1,3,2,0:T(8,128)(2,1)} %get-tuple-element.723, f32[2,17,512]{2,1,0:T(8,128)S(1)} %get-tuple-element.724, f32[2,17,512]{2,1,0:T(8,128)S(1)} %get-tuple-element.722, ...), kind=kOutput, calls=%fused_computation.27.clone.1 | convolution fusion | flops 1194328064 | bytes 58597376 | tf_op jit(solution)/shard_map/while/body/eval_jaxpr/sqhd,skhd->shqk/dot_general | solution.py:232
  1457.8 20.0 %fusion.65 = bf16[2,512,1088]{1,2,0:T(8,128)(2,1)} fusion(f32[2,512,1088]{1,2,0:T(8,128)} %copy-done.8, f32[2,512,1088]{1,2,0:T(8,128)} %fusion.101, bf16[2,512,4352]{2,1,0:T(8,128)(2,1)} %get-tuple-element.487, s32[]{:T(128)S(6)} %select_n.59, bf16[4352,1088]{0,1:T(8,128)(2,1)} %concatenate.18), kind=kOutput, calls=%fused_computation.106 | convolution fusion | flops 9719513088 | bytes 29523972 | tf_op jit(solution)/shard_map/slw,wv->slv/dot_general | solution.py:51
  1485.9 262.7 %reduce-scatter.34.cloned.1.call-done = bf16[2,512,2176]{1,2,0:T(8,128)(2,1)} async-done(((bf16[2,2048,2176]{1,2,0:T(8,128)(2,1)}), bf16[2,512,2176]{1,2,0:T(8,128)(2,1)}) %reduce-scatter.34.cloned.1.call-update) | async-done | bytes 4456464 | tf_op jit(solution)/shard_map/reduce_scatter | solution.py:263
  1763.5 15.1 fusion.156
  1780.3 20.7 %reduce-scatter.54.cloned.1.call-done = bf16[816,128]{1,0:T(8,128)(2,1)} async-done(((bf16[3264,128]{1,0:T(8,128)(2,1)}), bf16[816,128]{1,0:T(8,128)(2,1)}) %reduce-scatter.54.cloned.1.call-update) | async-done | bytes 208912
  1809.3 26.4 %reduce-scatter.36.cloned.1.call-done = bf16[16,272]{1,0:T(8,128)(2,1)} async-done(((bf16[128,272]{1,0:T(8,128)(2,1)}), bf16[16,272]{1,0:T(8,128)(2,1)}) %reduce-scatter.36.cloned.1.call-update) | async-done | bytes 8720 | tf_op jit(solution)/shard_map/reduce_scatter | solution.py:322
  1837.0 33.6 %reduce-scatter.38.cloned.1.call-done = bf16[16,816]{1,0:T(8,128)(2,1)} async-done(((bf16[128,816]{1,0:T(8,128)(2,1)}), bf16[16,816]{1,0:T(8,128)(2,1)}) %reduce-scatter.38.cloned.1.call-update) | async-done | bytes 26128 | tf_op jit(solution)/shard_map/reduce_scatter | solution.py:325
  (375 shorter events, 363.5 us)
Async XLA Ops:
  7.2 451.9 %copy-start = (bf16[128,4352]{1,0:T(8,128)(2,1)S(1)}, bf16[128,4352]{1,0:T(8,128)(2,1)}, u32[]{:S(2)}) copy-start(bf16[128,4352]{1,0:T(8,128)(2,1)} %param.38) | copy-start | bytes 3342340
  7.2 33.9 %all-gather.20.cloned.1.call-start = ((), (), s32[]{:S(2)}) async-start(), calls=%async_computation.31 | async-start | bytes 2506752 | tf_op jit(solution)/shard_map/all_gather | solution.py:77
  7.9 44.5 %copy-start.9 = (bf16[2,512,1088]{1,2,0:T(8,128)(2,1)S(1)}, bf16[2,512,1088]{1,2,0:T(8,128)(2,1)}, u32[]{:S(2)}) copy-start(bf16[2,512,1088]{1,2,0:T(8,128)(2,1)} %param.24) | copy-start | bytes 6684676
  7.9 173.6 %all-gather.10.cloned.1.call-start = ((), (), s32[]{:S(2)}) async-start(), calls=%async_computation.17 | async-start | bytes 9052160 | tf_op jit(solution)/shard_map/all_gather | solution.py:83
  50.5 160.8 %all-gather.18.cloned.1.call-start = ((), (), s32[]{:S(2)}) async-start(), calls=%async_computation.21 | async-start | bytes 2820096 | tf_op jit(solution)/shard_map/all_gather | solution.py:80
  51.3 420.0 %all-gather.22.cloned.1.call-start = ((), (), s32[]{:S(2)}) async-start(), calls=%async_computation.32 | async-start | bytes 3133440 | tf_op jit(solution)/shard_map/all_gather | solution.py:79
  51.8 611.6 %all-gather.12.cloned.1.call-start = ((), (), s32[]{:S(2)}) async-start(), calls=%async_computation.18 | async-start | bytes 22282240 | tf_op jit(solution)/shard_map/all_gather | solution.py:159
  61.7 132.3 %copy-start.29 = (bf16[2,16,3264]{2,0,1:T(2,128)(2,1)}, bf16[2,16,3264]{2,0,1:T(2,128)(2,1)S(1)}, u32[]{:S(2)}) copy-start(bf16[2,16,3264]{2,0,1:T(2,128)(2,1)S(1)} %convolution_convert_fusion.5) | copy-start | bytes 626692
  65.7 128.4 %copy-start.49 = (bf16[2,512,16]{1,2,0:T(8,128)(2,1)}, bf16[2,512,16]{1,2,0:T(8,128)(2,1)S(1)}, u32[]{:S(2)}) copy-start(bf16[2,512,16]{1,2,0:T(8,128)(2,1)S(1)} %convolution_convert_fusion.21) | copy-start | bytes 98308
  201.1 81.6 %copy-start.51 = (bf16[272,136]{0,1:T(8,128)(2,1)S(1)}, bf16[272,136]{0,1:T(8,128)(2,1)}, u32[]{:S(2)}) copy-start(bf16[272,136]{0,1:T(8,128)(2,1)} %param.28) | copy-start | bytes 221956
  201.1 251.1 %copy-start.46 = (s32[2]{0:T(128)S(1)}, s32[2]{0:T(128)}, u32[]{:S(2)}) copy-start(s32[2]{0:T(128)} %param.26) | copy-start | bytes 28
  201.1 691.7 %all-gather.14.cloned.1.call-start = ((), (), s32[]{:S(2)}) async-start(), calls=%async_computation.19 | async-start | bytes 3133440 | tf_op jit(solution)/shard_map/all_gather | solution.py:84
  211.4 67.0 %collective-permute-start = (bf16[1088,1088]{0,1:T(8,128)(2,1)}, bf16[1088,1088]{0,1:T(8,128)(2,1)}, u32[]{:S(2)}, u32[]{:S(2)}) collective-permute-start(bf16[1088,1088]{0,1:T(8,128)(2,1)} %all-gather.18.cloned.1.call-done), channel_id=1, source_target_pairs={{0,3},{1,0},{2,1},{3,2},{4,7},{5,4},{6,5},{7,6},{8,11},{9,8},{10,9... | collective-permute-start | bytes 7102472 | tf_op jit(solution)/shard_map/ppermute | solution.py:17
  278.4 173.6 %collective-permute-start.1 = (bf16[1088,1088]{0,1:T(8,128)(2,1)}, bf16[1088,1088]{0,1:T(8,128)(2,1)}, u32[]{:S(2)}, u32[]{:S(2)}) collective-permute-start(bf16[1088,1088]{0,1:T(8,128)(2,1)} %collective-permute-done), channel_id=1, source_target_pairs={{0,3},{1,0},{2,1},{3,2},{4,7},{5,4},{6,5},{7,6},{8,11},{9,8},{10,9... | collective-permute-start | bytes 7102472 | tf_op jit(solution)/shard_map/ppermute | solution.py:17
  293.9 168.3 %copy-start.18 = (bf16[2,512,1088]{1,2,0:T(8,128)(2,1)S(1)}, bf16[2,512,1088]{1,2,0:T(8,128)(2,1)}, u32[]{:S(2)}) copy-start(bf16[2,512,1088]{1,2,0:T(8,128)(2,1)} %param.41) | copy-start | bytes 6684676
  296.4 614.1 %all-gather.16.cloned.1.call-start = ((), (), s32[]{:S(2)}) async-start(), calls=%async_computation.20 | async-start | bytes 11837440 | tf_op jit(solution)/shard_map/all_gather | solution.py:85
  452.0 167.1 %collective-permute-start.2 = (bf16[1088,1088]{0,1:T(8,128)(2,1)}, bf16[1088,1088]{0,1:T(8,128)(2,1)}, u32[]{:S(2)}, u32[]{:S(2)}) collective-permute-start(bf16[1088,1088]{0,1:T(8,128)(2,1)} %collective-permute-done.1), channel_id=1, source_target_pairs={{0,3},{1,0},{2,1},{3,2},{4,7},{5,4},{6,5},{7,6},{8,11},{9,8},{10,9... | collective-permute-start | bytes 7102472 | tf_op jit(solution)/shard_map/ppermute | solution.py:17
  480.8 552.3 %reduce-scatter.66.cloned.1.call-start = ((), (), s32[]{:S(2)}) async-start(), calls=%async_computation.40 | async-start | bytes 348160
  635.2 28.2 %slice-start = ((bf16[2,512,3264]{1,2,0:T(8,128)(2,1)}), bf16[2,512,1088]{1,2,0:T(8,128)(2,1)S(1)}, s32[]{:S(2)}) async-start(bf16[2,512,3264]{1,2,0:T(8,128)(2,1)} %copy-done.2), calls=%async_computation.41 | async-start | bytes 4456448 | tf_op jit(solution)/shard_map/slice | solution.py:133
  884.6 13.7 copy-start.3
  910.5 25.4 %copy-start.27 = (bf16[2,16,4352]{2,0,1:T(2,128)(2,1)S(1)}, bf16[2,16,4352]{2,0,1:T(2,128)(2,1)}, u32[]{:S(2)}) copy-start(bf16[2,16,4352]{2,0,1:T(2,128)(2,1)} %copy-done.26) | copy-start | bytes 835588
  942.0 36.4 %copy-start.43 = (bf16[2,512,16]{1,2,0:T(8,128)(2,1)}, bf16[2,512,16]{1,2,0:T(8,128)(2,1)S(1)}, u32[]{:S(2)}) copy-start(bf16[2,512,16]{1,2,0:T(8,128)(2,1)S(1)} %convolution_convert_fusion.17) | copy-start | bytes 98308
  944.0 90.9 %reduce-scatter.60.cloned.1.call-start = ((), (), s32[]{:S(2)}) async-start(), calls=%async_computation.37 | async-start | bytes 348160
  989.1 17.4 copy-start.20
  989.1 47.5 %reduce-scatter.58.cloned.1.call-start = ((), (), s32[]{:S(2)}) async-start(), calls=%async_computation.36 | async-start | bytes 348160
  1014.2 41.4 %reduce-scatter.56.cloned.1.call-start = ((), (), s32[]{:S(2)}) async-start(), calls=%async_computation.35 | async-start | bytes 348160
  1018.9 65.8 %reduce-scatter.64.cloned.1.call-start = ((), (), s32[]{:S(2)}) async-start(), calls=%async_computation.39 | async-start | bytes 1392640
  1026.0 88.0 %reduce-scatter.62.cloned.1.call-start = ((), (), s32[]{:S(2)}) async-start(), calls=%async_computation.38 | async-start | bytes 1392640
  1033.1 444.7 %reduce-scatter.50.cloned.1.call-start = ((), (), s32[]{:S(2)}) async-start(), calls=%async_computation.30 | async-start | bytes 110592 | tf_op jit(solution)/shard_map/reduce_scatter | solution.py:343
  1034.8 444.3 %reduce-scatter.44.cloned.1.call-start = ((), (), s32[]{:S(2)}) async-start(), calls=%async_computation.27 | async-start | bytes 110592 | tf_op jit(solution)/shard_map/reduce_scatter | solution.py:334
  1036.6 443.9 %reduce-scatter.42.cloned.1.call-start = ((), (), s32[]{:S(2)}) async-start(), calls=%async_computation.26 | async-start | bytes 110592 | tf_op jit(solution)/shard_map/reduce_scatter | solution.py:331
  1038.3 443.5 %reduce-scatter.40.cloned.1.call-start = ((), (), s32[]{:S(2)}) async-start(), calls=%async_computation.25 | async-start | bytes 110592 | tf_op jit(solution)/shard_map/reduce_scatter | solution.py:328
  1057.2 29.4 %copy-start.34 = (bf16[2,16,1088]{2,0,1:T(2,128)(2,1)S(1)}, bf16[2,16,1088]{2,0,1:T(2,128)(2,1)}, u32[]{:S(2)}) copy-start(bf16[2,16,1088]{2,0,1:T(2,128)(2,1)} %convolution_convert_fusion.14) | copy-start | bytes 208900
  1057.2 425.9 %reduce-scatter.48.cloned.1.call-start = ((), (), s32[]{:S(2)}) async-start(), calls=%async_computation.29 | async-start | bytes 331776 | tf_op jit(solution)/shard_map/reduce_scatter | solution.py:340
  1086.6 398.0 %reduce-scatter.46.cloned.1.call-start = ((), (), s32[]{:S(2)}) async-start(), calls=%async_computation.28 | async-start | bytes 331776 | tf_op jit(solution)/shard_map/reduce_scatter | solution.py:337
  1115.9 632.7 %reduce-scatter.34.cloned.1.call-start = ((), (), s32[]{:S(2)}) async-start(), calls=%async_computation.22 | async-start | bytes 22282240 | tf_op jit(solution)/shard_map/reduce_scatter | solution.py:263
  1180.9 11.1 copy-start.5
  1192.1 9.6 copy-start.12
  1262.5 12.6 copy-start.5
  1345.6 12.4 copy-start.5
  1428.1 12.4 copy-start.5
  1452.7 325.9 %reduce-scatter.52.cloned.1.call-start = ((), (), s32[]{:S(2)}) async-start(), calls=%async_computation.33 | async-start | bytes 348160
  1457.8 297.0 %copy-start.28 = (bf16[2,512,17,64]{1,3,2,0:T(8,128)(2,1)}, bf16[2,512,17,64]{1,3,2,0:T(8,128)(2,1)S(1)}, u32[]{:S(2)}) copy-start(bf16[2,512,17,64]{1,3,2,0:T(8,128)(2,1)S(1)} %multiply_convert_fusion.1) | copy-start | bytes 6684676
  1457.8 290.8 %copy-start.30 = (bf16[2,16,3264]{2,0,1:T(2,128)(2,1)S(1)}, bf16[2,16,3264]{2,0,1:T(2,128)(2,1)}, u32[]{:S(2)}) copy-start(bf16[2,16,3264]{2,0,1:T(2,128)(2,1)} %copy-done.29) | copy-start | bytes 626692
  1754.8 46.2 %reduce-scatter.54.cloned.1.call-start = ((), (), s32[]{:S(2)}) async-start(), calls=%async_computation.34 | async-start | bytes 1044480
  1763.4 72.2 %reduce-scatter.36.cloned.1.call-start = ((), (), s32[]{:S(2)}) async-start(), calls=%async_computation.23 | async-start | bytes 110592 | tf_op jit(solution)/shard_map/reduce_scatter | solution.py:322
  1780.2 90.4 %reduce-scatter.38.cloned.1.call-start = ((), (), s32[]{:S(2)}) async-start(), calls=%async_computation.24 | async-start | bytes 258048 | tf_op jit(solution)/shard_map/reduce_scatter | solution.py:325
  1802.8 69.2 %copy-start.1 = (bf16[128,4352]{1,0:T(8,128)(2,1)S(1)}, bf16[128,4352]{1,0:T(8,128)(2,1)}, u32[]{:S(2)}) copy-start(bf16[128,4352]{1,0:T(8,128)(2,1)} %param.38) | copy-start | bytes 3342340
  (47 other events, 196.4 us)
Sparse Core Ops, SparseCore 0:
  9.9 31.1 all-gather.19
  50.7 130.8 all-gather.9
  183.5 27.8 all-gather.17
  213.1 30.7 all-gather.21
  245.4 417.9 all-gather.11
  664.8 53.9 all-gather.13
  720.4 166.0 all-gather.15
  944.1 20.7 reduce-scatter.65
  989.3 20.7 reduce-scatter.59
  1014.3 20.7 reduce-scatter.57
  1037.4 18.1 reduce-scatter.55
  1058.3 26.3 reduce-scatter.63
  1087.1 26.8 reduce-scatter.61
  1116.9 31.0 reduce-scatter.49
  1150.8 32.3 reduce-scatter.43
  1186.1 32.3 reduce-scatter.41
  1221.4 32.3 reduce-scatter.39
  1256.7 32.8 reduce-scatter.47
  1292.7 32.8 reduce-scatter.45
  1452.8 295.7 reduce-scatter.33
  1754.9 20.7 reduce-scatter.51
  1778.6 22.3 reduce-scatter.53
  1804.0 31.5 reduce-scatter.35
  1838.6 31.9 reduce-scatter.37
